TPU v7x, 128 devices: a whole 4x4x4 slice. The times are simulated.
128 devices in a mesh: row: 16 (over x, z_lo, core), col: 4 (over y), win: 2 (over z_hi).
Axes of the slice: x: 4, y: 4, z: 4 (z_hi: 2, z_lo: 2; z = z_hi * 2 + z_lo), core: 2. Of those that a mesh axis runs over, the one named last changes fastest.
Arguments:
- spectra: float32 [2, 2, 64, 2, 16384], P('win', None, ('row', 'col')), may hold values from -8 to 8
- tile_rows: int32 [8256], P(('row', 'col')), may hold values from 0 to 127, as said below
- tile_cols: int32 [8256], P(('row', 'col')), may hold values from 0 to 127, as said below
Outputs:
- cross: float32 [8256, 2, 2, 128, 128], P(('row', 'col'), None, None, 'win')
Inputs may be any that keep to these rules, and one draw needn't show every extreme that they name: tile_rows[k] <= tile_cols[k] for every k, and the pairs (tile_rows[k], tile_cols[k]) are all pairs of channel blocks with row block at most column block, each exactly once, in an order drawn from the seed. `tile_cols`: see tile_rows.
All inputs are finite; a program needn't handle non-finite values.
Results may differ from a plain program's by a relative error of at most 0.006.
Values may be sent and summed in bfloat16 or wider, within the bound.
A program may use at most 128 MiB of HBM per device.

v0:
```python
import jax
import jax.numpy as jnp
from jax import lax
from jax.sharding import PartitionSpec as P

BLOCK = 128


def whiten(spectra):
    power_sum = jnp.sum(spectra * spectra, axis=(1, 3), keepdims=True) / spectra.shape[1]
    return (spectra / jnp.maximum(jnp.sqrt(power_sum), 1.0)).astype(jnp.bfloat16)


def stack_pairs(source, tile_rows, tile_cols, norm_scale):
    gathered = lax.all_gather(source, ("row", "col"), axis=2, tiled=True)
    channel_count = gathered.shape[4]

    def per_freq(freq_slab):
        window_count = freq_slab.shape[0]
        blocks = freq_slab.reshape(window_count, 2, channel_count // BLOCK, BLOCK)
        left_block = jnp.take(blocks, tile_rows, axis=2)
        right_block = jnp.take(blocks, tile_cols, axis=2)
        real_part = jnp.einsum(
            "wpka,wpkb->kab", left_block, right_block, preferred_element_type=jnp.float32
        )
        imag_part = jnp.einsum(
            "wka,wkb->kab", left_block[:, 0], right_block[:, 1], preferred_element_type=jnp.float32
        )
        imag_part = imag_part - jnp.einsum(
            "wka,wkb->kab", left_block[:, 1], right_block[:, 0], preferred_element_type=jnp.float32
        )
        return jnp.stack([real_part, imag_part], axis=1) * norm_scale

    per_bin = lax.map(per_freq, gathered[0])
    return jnp.transpose(per_bin, (1, 0, 2, 3, 4))


def on_device(spectra, tile_rows, tile_cols):
    whitened = whiten(spectra)
    window_total = (
        spectra.shape[2] * lax.axis_size("row") * lax.axis_size("col") * lax.axis_size("win")
    )
    norm_scale = 1.0 / jnp.sqrt(jnp.float32(window_total))
    partial_value = stack_pairs(whitened, tile_rows, tile_cols, norm_scale)
    return lax.psum_scatter(
        partial_value.astype(jnp.bfloat16), "win", scatter_dimension=3, tiled=True
    ).astype(jnp.float32)


def solution(mesh):
    in_specs = (P("win", None, ("row", "col"), None, None), P(("row", "col")), P(("row", "col")))
    out_specs = P(("row", "col"), None, None, "win", None)
    return jax.shard_map(
        on_device, mesh=mesh, in_specs=in_specs, out_specs=out_specs, check_vma=False
    )
```

profile of v0, /device:TPU:1, one launch (start us, length us, event | category | flops | bytes accessed | tf_op | source)
XLA Modules:
  0.0 528.1 jit_solution(9032352772565153478)
XLA Ops:
  6.5 0.0 all-gather.2.cloned.1.call-start
  6.5 1.2 multiply_reduce_fusion
  7.7 1.7 fusion.3
  9.5 0.0 all-gather.2.cloned.1.call-update
  9.5 0.0 reduce-scatter.2.cloned.1.call-start
  9.5 168.8 %all-gather.2.cloned.1.call-done = bf16[1,2,64,2,16384]{4,3,1,0,2:T(2,128)(2,1)} async-done(((bf16[1,2,1,2,16384]{4,3,1,0,2:T(2,128)(2,1)}), bf16[1,2,64,2,16384]{4,3,1,0,2:T(2,128)(2,1)}) %all-gather.2.cloned.1.call-update) | async-done | bytes 8388624 | tf_op jit(solution)/shard_map/all_gather | solution.py:15
  178.4 136.1 %while.10 = (s32[]{:T(128)}, bf16[2,129,2,128,128]{4,3,2,0,1:T(8,128)(2,1)}, bf16[2,64,2,16384]{3,2,0,1:T(2,128)(2,1)}, s32[129]{0:T(256)}, s32[129]{0:T(256)}, /*index=5*/s32[]{:T(128)}) while((s32[]{:T(128)}, bf16[2,129,2,128,128]{4,3,2,0,1:T(8,128)(2,1)}, bf16[2,64,2,16384]{3,2,0,1:T(2,128)(2,1)}, s32[129]{0:T(256)}, s32[129]{0:T(256)}, ...), condition=%wide.region_2.0_spmd, body=%wide.region_1.3_spmd.sunk | while | flops 1101156608 | bytes 147769600 | solution.py:34
  178.4 0.7 compare_select_fusion.3
  179.1 10.4 %constant_dynamic-slice_fusion.2 = bf16[1,64,2,16384]{3,2,0,1:T(2,128)(2,1)} fusion(bf16[2,64,2,16384]{3,2,0,1:T(2,128)(2,1)} %get-tuple-element.106, s32[]{:T(128)} %get-tuple-element.98), kind=kLoop, calls=%fused_computation.21.clone.1 | loop fusion | bytes 8388612 | tf_op jit(solution)/shard_map/while/body/jit(dynamic_index_in_dim)/dynamic_slice | solution.py:34
  189.5 7.8 %reshape.86 = bf16[64,2,128,128]{3,2,1,0:T(8,128)(2,1)} reshape(bf16[1,64,2,16384]{3,2,0,1:T(2,128)(2,1)} %constant_dynamic-slice_fusion.2) | data formatting | bytes 8388608 | tf_op jit(solution)/shard_map/while/body/eval_jaxpr/reshape | solution.py:20
  197.3 6.8 %copy.46 = bf16[64,2,128,128]{3,0,2,1:T(8,128)(2,1)} copy(bf16[64,2,128,128]{3,2,1,0:T(8,128)(2,1)} %reshape.86) | data formatting | bytes 8388608 | tf_op jit(solution)/shard_map/while/body/eval_jaxpr/reshape | solution.py:20
  204.1 0.0 copy-start
  204.1 0.0 copy-start.1
  204.1 9.7 %gather_fusion = bf16[129,64,2,128]{3,1,2,0:T(8,128)(2,1)} fusion(bf16[64,2,128,128]{3,0,2,1:T(8,128)(2,1)} %copy.46, s32[1024]{0:T(1024)S(1)} %pad_clamp_fusion.4), kind=kCustom, calls=%fused_computation.1.clone.clone.1 | custom fusion | bytes 8454660 | tf_op jit(solution)/shard_map/while/body/eval_jaxpr/jit(_take)/gather | solution.py:22
  213.9 0.0 copy-done
  213.9 0.0 copy-done.1
  213.9 3.9 fusion.13
  217.8 9.7 %gather_fusion.1 = bf16[129,64,2,128]{3,1,2,0:T(8,128)(2,1)} fusion(bf16[64,2,128,128]{3,0,2,1:T(8,128)(2,1)} %copy.46, s32[1024]{0:T(1024)S(1)} %pad_clamp_fusion.5), kind=kCustom, calls=%fused_computation.clone.clone.1 | custom fusion | bytes 8454660 | tf_op jit(solution)/shard_map/while/body/eval_jaxpr/jit(_take)/gather | solution.py:21
  227.6 0.0 slice-start
  227.6 0.0 slice-start.1
  227.6 2.8 fusion.14
  230.4 0.7 slice-done
  231.0 0.0 slice-done.1
  231.0 1.6 convolution_bitcast_fusion.2
  232.6 1.3 fusion.15
  233.9 4.6 subtract_bitcast_fusion.2
  238.5 8.0 %copy_dynamic-update-slice_fusion.2 = bf16[2,129,2,128,128]{4,3,2,0,1:T(8,128)(2,1)} fusion(bf16[2,129,2,128,128]{4,3,2,0,1:T(8,128)(2,1)} %get-tuple-element.99, s32[]{:T(128)} %get-tuple-element.98, f32[1,129,1,128,128]{4,3,1,2,0:T(8,128)} %subtract_bitcast_fusion.2, f32[1,129,1,128,128]{4,3,1,2,0:T(8,128)S(1)} %convolution_bitcast_fusion.2), kind=kLoop, calls=%fused_computation.3.clone.1 | loop fusion | flops 12681216 | bytes 25362944 | tf_op jit(solution)/shard_map/while/body/jit(dynamic_update_index_in_dim)/dynamic_update_slice | solution.py:34
  246.5 0.7 compare_select_fusion.3
  247.2 10.4 %constant_dynamic-slice_fusion.2 = bf16[1,64,2,16384]{3,2,0,1:T(2,128)(2,1)} fusion(bf16[2,64,2,16384]{3,2,0,1:T(2,128)(2,1)} %get-tuple-element.106, s32[]{:T(128)} %get-tuple-element.98), kind=kLoop, calls=%fused_computation.21.clone.1 | loop fusion | bytes 8388612 | tf_op jit(solution)/shard_map/while/body/jit(dynamic_index_in_dim)/dynamic_slice | solution.py:34
  257.5 7.8 %reshape.86 = bf16[64,2,128,128]{3,2,1,0:T(8,128)(2,1)} reshape(bf16[1,64,2,16384]{3,2,0,1:T(2,128)(2,1)} %constant_dynamic-slice_fusion.2) | data formatting | bytes 8388608 | tf_op jit(solution)/shard_map/while/body/eval_jaxpr/reshape | solution.py:20
  265.4 6.8 %copy.46 = bf16[64,2,128,128]{3,0,2,1:T(8,128)(2,1)} copy(bf16[64,2,128,128]{3,2,1,0:T(8,128)(2,1)} %reshape.86) | data formatting | bytes 8388608 | tf_op jit(solution)/shard_map/while/body/eval_jaxpr/reshape | solution.py:20
  272.2 0.0 copy-start
  272.2 0.0 copy-start.1
  272.2 9.7 %gather_fusion = bf16[129,64,2,128]{3,1,2,0:T(8,128)(2,1)} fusion(bf16[64,2,128,128]{3,0,2,1:T(8,128)(2,1)} %copy.46, s32[1024]{0:T(1024)S(1)} %pad_clamp_fusion.4), kind=kCustom, calls=%fused_computation.1.clone.clone.1 | custom fusion | bytes 8454660 | tf_op jit(solution)/shard_map/while/body/eval_jaxpr/jit(_take)/gather | solution.py:22
  281.9 0.0 copy-done
  281.9 0.0 copy-done.1
  282.0 3.9 fusion.13
  285.9 9.7 %gather_fusion.1 = bf16[129,64,2,128]{3,1,2,0:T(8,128)(2,1)} fusion(bf16[64,2,128,128]{3,0,2,1:T(8,128)(2,1)} %copy.46, s32[1024]{0:T(1024)S(1)} %pad_clamp_fusion.5), kind=kCustom, calls=%fused_computation.clone.clone.1 | custom fusion | bytes 8454660 | tf_op jit(solution)/shard_map/while/body/eval_jaxpr/jit(_take)/gather | solution.py:21
  295.6 0.0 slice-start
  295.6 0.0 slice-start.1
  295.6 2.8 fusion.14
  298.4 0.7 slice-done
  299.1 0.0 slice-done.1
  299.1 1.6 convolution_bitcast_fusion.2
  300.6 1.3 fusion.15
  302.0 4.6 subtract_bitcast_fusion.2
  306.6 8.0 %copy_dynamic-update-slice_fusion.2 = bf16[2,129,2,128,128]{4,3,2,0,1:T(8,128)(2,1)} fusion(bf16[2,129,2,128,128]{4,3,2,0,1:T(8,128)(2,1)} %get-tuple-element.99, s32[]{:T(128)} %get-tuple-element.98, f32[1,129,1,128,128]{4,3,1,2,0:T(8,128)} %subtract_bitcast_fusion.2, f32[1,129,1,128,128]{4,3,1,2,0:T(8,128)S(1)} %convolution_bitcast_fusion.2), kind=kLoop, calls=%fused_computation.3.clone.1 | loop fusion | flops 12681216 | bytes 25362944 | tf_op jit(solution)/shard_map/while/body/jit(dynamic_update_index_in_dim)/dynamic_update_slice | solution.py:34
  314.5 0.0 reduce-scatter.2.cloned.1.call-update
  314.5 194.8 %reduce-scatter.2.cloned.1.call-done = bf16[129,2,2,64,128]{4,3,2,1,0:T(8,128)(2,1)} async-done(((bf16[129,2,2,128,128]{4,3,2,1,0:T(8,128)(2,1)}), bf16[129,2,2,64,128]{4,3,2,1,0:T(8,128)(2,1)}) %reduce-scatter.2.cloned.1.call-update) | async-done | bytes 8454160 | tf_op jit(solution)/shard_map/reduce_scatter | solution.py:45
  509.4 11.9 %convert_element_type.15 = f32[129,2,2,64,128]{4,3,2,1,0:T(8,128)} convert(bf16[129,2,2,64,128]{4,3,2,1,0:T(8,128)(2,1)} %reduce-scatter.2.cloned.1.call-done) | non-fusion elementwise | flops 4227072 | bytes 25362432 | tf_op jit(solution)/shard_map/convert_element_type | solution.py:47
  (10 shorter events, 0.1 us)
Async XLA Ops:
  6.5 171.8 %all-gather.2.cloned.1.call-start = ((), (), s32[]{:S(2)}) async-start(), calls=%async_computation.1 | async-start | bytes 8519680 | tf_op jit(solution)/shard_map/all_gather | solution.py:15
  9.5 499.9 %reduce-scatter.2.cloned.1.call-start = ((), (), s32[]{:S(2)}) async-start(), calls=%async_computation.2 | async-start | bytes 25362432 | tf_op jit(solution)/shard_map/reduce_scatter | solution.py:45
  204.1 9.8 %copy-start = (s32[129]{0:T(256)S(1)}, s32[129]{0:T(256)}, u32[]{:S(2)}) copy-start(s32[129]{0:T(256)} %get-tuple-element.107) | copy-start | bytes 1552 | tf_op jit(solution)/shard_map/while
  204.1 9.8 %copy-start.1 = (s32[129]{0:T(256)S(1)}, s32[129]{0:T(256)}, u32[]{:S(2)}) copy-start(s32[129]{0:T(256)} %get-tuple-element.108) | copy-start | bytes 1552 | tf_op jit(solution)/shard_map/while
  227.6 3.5 slice-start
  227.6 3.5 slice-start.1
  272.2 9.8 %copy-start = (s32[129]{0:T(256)S(1)}, s32[129]{0:T(256)}, u32[]{:S(2)}) copy-start(s32[129]{0:T(256)} %get-tuple-element.107) | copy-start | bytes 1552 | tf_op jit(solution)/shard_map/while
  272.2 9.8 %copy-start.1 = (s32[129]{0:T(256)S(1)}, s32[129]{0:T(256)}, u32[]{:S(2)}) copy-start(s32[129]{0:T(256)} %get-tuple-element.108) | copy-start | bytes 1552 | tf_op jit(solution)/shard_map/while
  295.6 3.5 slice-start
  295.6 3.5 slice-start.1
Sparse Core Ops, SparseCore 0:
  9.6 168.7 all-gather.1
  314.7 194.6 reduce-scatter.1
where the time goes:
time: 529 us; the launch traced here: 528 us
  waiting for transfers between devices  364 us (69%)
  local copies, waits for them, and re-layouts  90.3 us (17%)
  other arithmetic  45.6 us (9%)
  matrix products  14.9 us (3%)
  between operations  13.4 us (3%)
    reduce_scatter x1, waiting for transfers between devices, on_device(): lax.psum_scatter(partial_value.astype(jnp.bfloat16), 'win', scatter_dimen...  195 us
    all_gather x1, waiting for transfers between devices, stack_pairs(): gathered = lax.all_gather(source, ('row', 'col'), axis=2, tiled=True)  169 us
    reshape x4, local copies, waits for them, and re-layouts, per_freq(): blocks = freq_slab.reshape(window_count, 2, channel_count // BLOCK, BLOCK)  29.3 us
    dynamic_slice x2, local copies, waits for them, and re-layouts, stack_pairs(): per_bin = lax.map(per_freq, gathered[0])  20.7 us
    gather x2, local copies, waits for them, and re-layouts, per_freq(): right_block = jnp.take(blocks, tile_cols, axis=2)  19.5 us
    gather x2, local copies, waits for them, and re-layouts, per_freq(): left_block = jnp.take(blocks, tile_rows, axis=2)  19.4 us
    dynamic_update_slice x2, other arithmetic, stack_pairs(): per_bin = lax.map(per_freq, gathered[0])  15.9 us
    convert_element_type x1, other arithmetic, on_device(): return lax.psum_scatter(partial_value.astype(jnp.bfloat16), 'win', scatte...  11.9 us
  transfers between devices with their start and end apart: 2, of which 2 were waited for; matrix products, arithmetic and copies ran while one was open for 0% of the time, Pallas kernels for 0%

commit v1 on v0

v1 whole, which is shorter than its diff:
```python
import functools

import jax
import jax.numpy as jnp
from jax import lax
from jax.experimental import pallas as pl
from jax.experimental.pallas import tpu as pltpu
from jax.sharding import PartitionSpec as P

MESH = pl.DeviceIdType.MESH
BLOCK = 128
GATHERED = (2, 2, 4, 2, 8, 2, 4, 2, 16, 128)
STREAMS = (
    (0, 0, 3, "xyz"),
    (0, 3, 3, "yzx"),
    (0, 6, 2, "zxy"),
    (1, 0, 3, "xyz"),
    (1, 3, 2, "yzx"),
    (1, 5, 3, "zxy"),
)
UNROLL = 43


def whiten(spectra):
    power_sum = jnp.sum(spectra * spectra, axis=(1, 3), keepdims=True) / spectra.shape[1]
    return (spectra / jnp.maximum(jnp.sqrt(power_sum), 1.0)).astype(jnp.bfloat16)


def gather_kernel(
    src_ref, g, landed, spread, a2a_send, a2a_recv, send_sem, recv_sem, pass_send, pass_recv
):
    row, y, zh = lax.axis_index("row"), lax.axis_index("col"), lax.axis_index("win")
    x, zl, core = row // 4, (row // 2) % 2, row % 2
    here = {"x": x, "y": y, "z": zh * 2 + zl}

    def device(at, at_core):
        z = at["z"]
        return (at["x"] * 4 + (z % 2) * 2 + at_core, at["y"], z // 2)

    def shifted(axis, by):
        return here | {axis: (here[axis] + by) % 4}

    partner = device(here, 1 - core)
    me = (core * 4 + y) * 2 + zl

    def member(by):
        m = (me + by) % 16
        return m, (x * 4 + (m % 2) * 2 + m // 8, (m // 2) % 4, zh)

    barrier = pltpu.get_barrier_semaphore()
    others = [member(by)[1] for by in range(1, 16)]
    others += [device(shifted("x", 1), core), device(shifted("x", -1), core)]
    outer_z = here | {"z": (here["z"] + jnp.where(zl == 0, 3, 1)) % 4}
    others += [device(outer_z, core)]
    for other in others:
        pl.semaphore_signal(barrier, inc=1, device_id=other, device_id_type=MESH)
    pl.semaphore_wait(barrier, len(others))

    def swap(by):
        m, where = member(by)
        return pltpu.make_async_remote_copy(
            src_ref=src_ref.at[m],
            dst_ref=landed.at[me],
            send_sem=a2a_send.at[by],
            recv_sem=a2a_recv.at[by],
            device_id=where,
            device_id_type=MESH,
        )

    swaps = [swap(by) for by in range(1, 16)]
    for copy in swaps:
        copy.start()
    own = pltpu.make_async_copy(src_ref.at[me], landed.at[me], a2a_recv.at[0])
    own.start()
    own.wait()
    for copy in swaps:
        copy.wait_recv()
    for f in range(2):
        for p in range(2):
            for s in range(16):
                spread[f, p, pl.ds(s * 8, 8), :] = landed[s, f, p].astype(jnp.float32)
    for f in range(2):
        for p in range(2):
            for b in range(8):
                windows = spread[f, p, pl.ds(b, 16, stride=8), :]
                g[f, core, y, zl, b, p, x, zh] = windows.astype(jnp.bfloat16)

    every = slice(None)

    def box(stream, phase, at, part):
        f, b0, bn, order = STREAMS[stream]
        full = order[:phase]
        ys = every if "y" in full else at["y"]
        xs = every if "x" in full else at["x"]
        zls, zhs = (every, every) if "z" in full else (at["z"] % 2, at["z"] // 2)
        return g.at[f, core, ys, zls, pl.ds(b0, bn), part, xs, zhs]

    def ring(stream, phase, slot):
        axis = STREAMS[stream][3][phase]
        way, whose, part = ((1, 0, 0), (-1, 0, 1), (1, 0, 1), (-1, 0, 0), (1, -1, 0), (-1, 1, 1))[slot]
        ref = box(stream, phase, shifted(axis, whose), part)
        return pltpu.make_async_remote_copy(
            src_ref=ref,
            dst_ref=ref,
            send_sem=send_sem.at[stream, phase],
            recv_sem=recv_sem.at[stream, phase, slot],
            device_id=device(shifted(axis, way), core),
            device_id_type=MESH,
        )

    def arrived(stream, phase, slot):
        axis = STREAMS[stream][3][phase]
        way, whose, part = ((1, 0, 0), (-1, 0, 1), (1, 0, 1), (-1, 0, 0), (1, -1, 0), (-1, 1, 1))[slot]
        ref = box(stream, phase, shifted(axis, whose - way), part)
        pltpu.make_async_copy(ref, ref, recv_sem.at[stream, phase, slot]).wait()
        return ref

    def hand_over(stream, ref):
        pltpu.make_async_remote_copy(
            src_ref=ref,
            dst_ref=ref,
            send_sem=pass_send.at[stream],
            recv_sem=pass_recv.at[stream],
            device_id=partner,
            device_id_type=MESH,
        ).start()

    def start(stream, phase):
        for slot in range(4):
            ring(stream, phase, slot).start()
        if phase == 0:
            for part in range(2):
                hand_over(stream, box(stream, 0, here, part))

    def relay(stream, phase):
        for slot in range(2):
            ref = arrived(stream, phase, slot)
            ring(stream, phase, slot + 4).start()
            hand_over(stream, ref)

    def finish(stream, phase):
        for slot in range(2, 6):
            hand_over(stream, arrived(stream, phase, slot))

    early, late = range(3), range(3, 6)
    for group in (early, late):
        for s in group:
            start(s, 0)
    for group in (early, late):
        for s in group:
            relay(s, 0)
    for group in (early, late):
        for s in group:
            finish(s, 0)
            start(s, 1)
    for phase in (1, 2):
        for group in (early, late):
            for s in group:
                relay(s, phase)
            for s in group:
                finish(s, phase)
                if phase == 1:
                    start(s, 2)

    for copy in swaps:
        copy.wait_send()
    for s, (f, b0, bn, order) in enumerate(STREAMS):
        for phase in range(3):
            xs = slice(0, 1) if phase == 0 else every
            zs = slice(0, 1) if phase < 2 else every
            ref = g.at[f, core, pl.ds(0, 3), zs, pl.ds(b0, bn), :, xs, zs]
            pltpu.make_async_copy(ref, ref, send_sem.at[s, phase]).wait()
        ref = g.at[f, core, :, :, pl.ds(b0, bn)]
        pltpu.make_async_copy(ref, ref, pass_send.at[s]).wait()
        ref = g.at[f, 1 - core, :, :, pl.ds(b0, bn)]
        pltpu.make_async_copy(ref, ref, pass_recv.at[s]).wait()


def gather(source):
    return pl.pallas_call(
        gather_kernel,
        out_shape=pltpu.VMEM(GATHERED, jnp.bfloat16),
        in_specs=[pl.BlockSpec(memory_space=pltpu.VMEM)],
        out_specs=pl.BlockSpec(memory_space=pltpu.VMEM),
        scratch_shapes=[
            pltpu.VMEM((16, 2, 2, 8, BLOCK), jnp.bfloat16),
            pltpu.VMEM((2, 2, BLOCK, BLOCK), jnp.float32),
            pltpu.SemaphoreType.DMA((16,)),
            pltpu.SemaphoreType.DMA((16,)),
            pltpu.SemaphoreType.DMA((6, 3)),
            pltpu.SemaphoreType.DMA((6, 3, 6)),
            pltpu.SemaphoreType.DMA((6,)),
            pltpu.SemaphoreType.DMA((6,)),
        ],
        compiler_params=pltpu.CompilerParams(
            collective_id=0, has_side_effects=True, vmem_limit_bytes=32 << 20
        ),
    )(source)


def stack_kernel(rows_ref, cols_ref, g_ref, out_ref, held, sem):
    win = lax.axis_index("win")
    tiles = rows_ref.shape[0]
    norm = 1.0 / jnp.sqrt(jnp.float32(BLOCK))
    steps = tiles // UNROLL

    def put(f, step):
        slot = (f * steps + step) % 2
        return pltpu.make_async_copy(
            held.at[slot], out_ref.at[pl.ds(step * UNROLL, UNROLL), f], sem.at[slot]
        )

    for f in range(2):

        def body(step, carry):
            slot = (f * steps + step) % 2

            @pl.when(f * steps + step >= 2)
            def _():
                put(f, step).wait()

            for u in range(UNROLL):
                k = step * UNROLL + u
                turned = g_ref[f, rows_ref[k]].T
                left = jnp.where(win == 0, turned[:64], turned[64:])
                crossed = jnp.concatenate([-left[:, 128:], left[:, :128]], axis=1)
                both = jnp.dot(
                    jnp.concatenate([left, crossed], axis=0),
                    g_ref[f, cols_ref[k]],
                    preferred_element_type=jnp.float32,
                )
                both = both * norm
                held[slot, u, 0] = both[:64]
                held[slot, u, 1] = both[64:]
            put(f, step).start()
            return carry

        lax.fori_loop(0, steps, body, 0)
    put(1, steps - 2).wait()
    put(1, steps - 1).wait()


def stack_pairs(gathered, tile_rows, tile_cols):
    tiles = tile_rows.shape[0]
    return pl.pallas_call(
        stack_kernel,
        out_shape=jax.ShapeDtypeStruct((tiles, 2, 2, 64, BLOCK), jnp.float32),
        in_specs=[pl.BlockSpec(memory_space=pltpu.SMEM)] * 2 + [pl.BlockSpec(memory_space=pltpu.VMEM)],
        out_specs=pl.BlockSpec(memory_space=pl.ANY),
        scratch_shapes=[
            pltpu.VMEM((2, UNROLL, 2, 64, BLOCK), jnp.float32),
            pltpu.SemaphoreType.DMA((2,)),
        ],
        compiler_params=pltpu.CompilerParams(vmem_limit_bytes=30 << 20),
    )(tile_rows, tile_cols, gathered)


def on_device(spectra, tile_rows, tile_cols):
    whitened = whiten(spectra)[0, :, 0].reshape(2, 2, 16, 8, BLOCK)
    gathered = gather(jnp.transpose(whitened, (2, 0, 1, 3, 4)))
    return stack_pairs(gathered.reshape(2, 128, 256, BLOCK), tile_rows, tile_cols)


def solution(mesh):
    in_specs = (P("win", None, ("row", "col"), None, None), P(("row", "col")), P(("row", "col")))
    out_specs = P(("row", "col"), None, None, "win", None)
    return jax.shard_map(
        on_device, mesh=mesh, in_specs=in_specs, out_specs=out_specs, check_vma=False
    )
```

time: 529 us -> 70.3 us (0.13)
  waiting for transfers between devices: 364 us -> 0 us
  local copies, waits for them, and re-layouts: 90.3 us -> 0.14 us
  Pallas kernels: 0 us -> 67.7 us
  other arithmetic: 45.6 us -> 2.28 us
  matrix products: 14.9 us -> 0 us
  between operations: 13.4 us -> 0.05 us
    reduce_scatter x1 -> x0, waiting for transfers between devices: 195 us -> none  [on_device(): lax.psum_scatter(partial_value.astype(jnp.bfloat16), 'win', scatter_dimen...]
    all_gather x1 -> x0, waiting for transfers between devices: 169 us -> none  [stack_pairs(): gathered = lax.all_gather(source, ('row', 'col'), axis=2, tiled=True)]
    pallas_call x0 -> x2, Pallas kernels: none -> 67.7 us  [the longest x1 58.5 us: gather(): pl.pallas_call(gather_kernel, out_shape=pltpu.VMEM(GATHERED, jnp.bfloat16...]
    gather x4 -> x0, local copies, waits for them, and re-layouts: 38.9 us -> none  [the longest x2 19.5 us: per_freq(): right_block = jnp.take(blocks, tile_cols, axis=2)]
    reshape x4 -> x0, local copies, waits for them, and re-layouts: 29.3 us -> none  [per_freq(): blocks = freq_slab.reshape(window_count, 2, channel_count // BLOCK, BLOCK)]
    dynamic_slice x2 -> x0, local copies, waits for them, and re-layouts: 20.7 us -> none  [stack_pairs(): per_bin = lax.map(per_freq, gathered[0])]
    dynamic_update_slice x2 -> x0, other arithmetic: 15.9 us -> none  [stack_pairs(): per_bin = lax.map(per_freq, gathered[0])]
    dot_general x6 -> x0, matrix products: 14.9 us -> none  [the longest x2 9.17 us: per_freq(): jnp.einsum('wka,wkb->kab', left_block[:, 1], right_block[:, 0], preferred...]
  transfers between devices with their start and end apart: 2 -> 0, of which waited for: 2 -> 0; matrix products, arithmetic and copies ran while one was open for 0% -> 0% of each run, Pallas kernels for 0% -> 0%
where the time goes in v1:
time: 70.3 us; the launch traced here: 70.2 us
  Pallas kernels  67.7 us (96%)
  other arithmetic  2.28 us (3%)
    pallas_call x1, Pallas kernels, gather(): pl.pallas_call(gather_kernel, out_shape=pltpu.VMEM(GATHERED, jnp.bfloat16...  58.5 us
    pallas_call x1, Pallas kernels, stack_pairs(): pl.pallas_call(stack_kernel, out_shape=jax.ShapeDtypeStruct((tiles, 2, 2,...  9.19 us

profile of v1, /device:TPU:1, one launch (start us, length us, event | category | flops | bytes accessed | tf_op | source)
XLA Modules:
  0.0 70.2 jit_solution(1528998441898406082)
XLA Ops:
  0.0 0.0 copy-start.1
  0.0 0.0 copy-start
  0.0 1.2 %multiply_reduce_fusion = f32[16384]{0:T(1024)S(1)} fusion(f32[1,2,1,2,16384]{4,3,2,1,0:T(2,128)} %param.3), kind=kLoop, calls=%fused_computation | loop fusion | flops 114688 | bytes 327680 | tf_op jit(solution)/shard_map/reduce_sum | solution.py:25
  1.2 1.1 %divide_convert_fusion = bf16[1,2,1,2,16384]{4,3,2,1,0:T(2,128)(2,1)S(1)} fusion(f32[1,2,1,2,16384]{4,3,2,1,0:T(2,128)} %param.3, f32[16384]{0:T(1024)S(1)} %sqrt_maximum_fusion), kind=kLoop, calls=%fused_computation.1 | loop fusion | flops 131072 | bytes 458752 | tf_op jit(solution)/shard_map/convert_element_type | solution.py:26
  2.3 0.1 reshape_squeeze.3
  2.4 58.5 %shard_map.37 = bf16[2,2,4,2,8,2,4,2,16,128]{9,8,7,6,5,4,3,2,1,0:T(8,128)(2,1)S(1)} custom-call(bf16[16,2,2,8,128]{4,3,2,1,0:T(8,128)(2,1)S(1)} %bitcast.5), custom_call_target="tpu_custom_call" | custom-call | tf_op jit(solution)/shard_map/pallas_call | solution.py:180
  61.0 0.0 copy-done.1
  61.0 0.0 copy-done
  61.0 9.2 %shard_map.38 = f32[129,2,2,64,128]{4,3,2,1,0:T(8,128)} custom-call(s32[129]{0:T(256)S(1)} %copy-done, s32[129]{0:T(256)S(1)} %copy-done.1, bf16[2,128,256,128]{3,2,1,0:T(8,128)(2,1)S(1)} %bitcast.4), custom_call_target="tpu_custom_call" | custom-call | tf_op jit(solution)/shard_map/pallas_call | solution.py:245
  (2 shorter events, 0.1 us)
Async XLA Ops:
  0.0 61.0 %copy-start.1 = (s32[129]{0:T(256)S(1)}, s32[129]{0:T(256)}, u32[]{:S(2)}) copy-start(s32[129]{0:T(256)} %cols_ref.1) | copy-start | bytes 1552
  0.0 61.0 %copy-start = (s32[129]{0:T(256)S(1)}, s32[129]{0:T(256)}, u32[]{:S(2)}) copy-start(s32[129]{0:T(256)} %rows_ref.1) | copy-start | bytes 1552

commit v2 on v1

v2 whole, which is shorter than its diff:
```python
import functools
import heapq

import jax
import jax.numpy as jnp
from jax import lax
from jax.experimental import pallas as pl
from jax.experimental.pallas import tpu as pltpu
from jax.sharding import PartitionSpec as P

MESH = pl.DeviceIdType.MESH
BLOCK = 128
GATHERED = (2, 4, 32, 2, 4, 4, 8, BLOCK)
STREAMS = ((0, 11, "xyz"), (11, 11, "yzx"), (22, 10, "zxy"))
OFFSETS = (0, 1, -1, 2)
SLOTS = ((1, 0, 0), (-1, 0, 1), (1, 0, 1), (-1, 0, 0), (1, -1, 0), (-1, 1, 1))
PIECES = tuple(
    (stream, phase, offset)
    for stream in range(3)
    for phase in range(3)
    for offset in (OFFSETS if phase else (0,))
)
UNROLL = 43


def plan(hop=1.6, rate=46.5e3):
    needs = {}
    for piece in PIECES:
        stream, phase, offset = piece
        for part in range(2):
            if phase == 0 or (phase == 1 and offset == 0):
                need = set()
            elif phase == 1:
                need = {((stream, 0, 0), offset, part)}
            elif offset == 0:
                need = {((stream, 0, 0), by, part) for by in OFFSETS[1:]}
            else:
                need = {((stream, 1, by), offset, part) for by in OFFSETS}
            needs[piece, part] = need
    free, heap, have, started = {}, [], set(), set()

    def send(piece, slot, now):
        stream, phase, offset = piece
        _, units, order = STREAMS[stream]
        link = (order[phase], SLOTS[slot][0])
        size = units * 2048 * (4 if phase == 2 else 1)
        begin = max(now, free.get(link, 0.0))
        free[link] = begin + size / rate
        heapq.heappush(heap, (free[link] + hop, len(started), piece, slot))
        started.add((piece, slot))

    def ready(now):
        out = []
        for phase in range(3):
            for slot in range(4):
                for piece in PIECES:
                    if piece[1] == phase and (piece, slot) not in started:
                        if needs[piece, SLOTS[slot][2]] <= have:
                            send(piece, slot, now)
                            out.append((piece, slot))
        return out

    steps = [(None, ready(0.0))]
    while heap:
        now, _, piece, slot = heapq.heappop(heap)
        way, whose, part = SLOTS[slot]
        out = []
        if slot < 2:
            send(piece, slot + 4, now)
            out.append((piece, slot + 4))
        have.add((piece, {-1: -1, 1: 1, -2: 2, 2: 2}[whose - way], part))
        steps.append(((piece, slot), out + ready(now)))
    return steps, now


def gather_kernel(x_ref, g, raw, source, landed, spread, load, a2a_send, a2a_recv, sent, got, passed, taken):
    row, y, zh = lax.axis_index("row"), lax.axis_index("col"), lax.axis_index("win")
    x, zl, core = row // 4, (row // 2) % 2, row % 2
    z = zh * 2 + zl
    here = {"x": x, "y": y, "z": z}

    def device(at, at_core):
        return (at["x"] * 4 + (at["z"] % 2) * 2 + at_core, at["y"], at["z"] // 2)

    def shifted(axis, by):
        return here | {axis: (here[axis] + by) % 4}

    me = core * 4 + y

    def member(by):
        m = (me + by) % 8
        return m, device(here | {"y": m % 4}, m // 4)

    fetch = pltpu.make_async_copy(x_ref, raw, load)
    fetch.start()
    barrier = pltpu.get_barrier_semaphore()
    others = [member(by)[1] for by in range(1, 8)]
    others += [device(shifted(axis, by), core) for axis in "xz" for by in (1, -1)]
    for other in others:
        pl.semaphore_signal(barrier, inc=1, device_id=other, device_id_type=MESH)
    fetch.wait()
    for m in range(8):
        values = [[raw[f, pl.ds(m * 32 + p, 16, stride=2), :] for p in range(2)] for f in range(2)]
        power = sum(v * v for pair in values for v in pair) / 2
        scale = jnp.maximum(jnp.sqrt(power), 1.0)
        for f in range(2):
            for p in range(2):
                source[m, f, p] = (values[f][p] / scale).astype(jnp.bfloat16)
    pl.semaphore_wait(barrier, len(others))

    def swap(by):
        m, where = member(by)
        return pltpu.make_async_remote_copy(
            src_ref=source.at[m],
            dst_ref=landed.at[me],
            send_sem=a2a_send.at[by],
            recv_sem=a2a_recv.at[by],
            device_id=where,
            device_id_type=MESH,
        )

    swaps = [swap(by) for by in range(1, 8)]
    for copy in swaps:
        copy.start()
    own = pltpu.make_async_copy(source.at[me], landed.at[me], a2a_recv.at[0])
    own.start()
    own.wait()
    for copy in swaps:
        copy.wait_recv()
    for f in range(2):
        for p in range(2):
            for s in range(8):
                spread[f, p, pl.ds(s * 16, 16), :] = landed[s, f, p].astype(jnp.float32)
    for f in range(2):
        for p in range(2):
            for b in range(16):
                windows = spread[f, p, pl.ds(b, 8, stride=16), :]
                g[core, y, b * 2 + f, p, x, z] = windows.astype(jnp.bfloat16)

    every = slice(None)

    def box(piece, by, part):
        stream, phase, offset = piece
        first, units, order = STREAMS[stream]
        at = dict(here)
        at[order[phase]] = (here[order[phase]] + by) % 4
        if phase:
            at[order[phase - 1]] = (here[order[phase - 1]] + offset) % 4
        if phase == 2:
            at[order[0]] = every
        return g.at[core, at["y"], pl.ds(first, units), part, at["x"], at["z"]]

    def index(piece):
        return PIECES.index(piece)

    def launch(piece, slot):
        way, whose, part = SLOTS[slot]
        ref = box(piece, whose, part)
        pltpu.make_async_remote_copy(
            src_ref=ref,
            dst_ref=ref,
            send_sem=sent.at[piece[0], piece[1]],
            recv_sem=got.at[index(piece), slot],
            device_id=device(shifted(STREAMS[piece[0]][2][piece[1]], way), core),
            device_id_type=MESH,
        ).start()

    def hand_over(ref):
        pltpu.make_async_remote_copy(
            src_ref=ref,
            dst_ref=ref,
            send_sem=passed,
            recv_sem=taken,
            device_id=device(here, 1 - core),
            device_id_type=MESH,
        ).start()

    for received, copies in plan()[0]:
        if received is not None:
            piece, slot = received
            way, whose, part = SLOTS[slot]
            ref = box(piece, whose - way, part)
            pltpu.make_async_copy(ref, ref, got.at[index(piece), slot]).wait()
        for copy in copies:
            launch(*copy)
        hand_over(g.at[core, y, :, :, x, z] if received is None else ref)

    for copy in swaps:
        copy.wait_send()
    for s, (first, units, _) in enumerate(STREAMS):
        for phase in range(3):
            xs = slice(0, 1) if phase == 0 else every
            zs = slice(0, 1) if phase < 2 else every
            ref = g.at[core, pl.ds(0, 3), pl.ds(first, units), :, xs, zs]
            pltpu.make_async_copy(ref, ref, sent.at[s, phase]).wait()
    pltpu.make_async_copy(g.at[core], g.at[core], passed).wait()
    pltpu.make_async_copy(g.at[1 - core], g.at[1 - core], taken).wait()


def gather(spectra):
    return pl.pallas_call(
        gather_kernel,
        out_shape=pltpu.VMEM(GATHERED, jnp.bfloat16),
        in_specs=[pl.BlockSpec(memory_space=pltpu.HBM)],
        out_specs=pl.BlockSpec(memory_space=pltpu.VMEM),
        scratch_shapes=[
            pltpu.VMEM((2, 256, BLOCK), jnp.float32),
            pltpu.VMEM((8, 2, 2, 16, BLOCK), jnp.bfloat16),
            pltpu.VMEM((8, 2, 2, 16, BLOCK), jnp.bfloat16),
            pltpu.VMEM((2, 2, BLOCK, BLOCK), jnp.float32),
            pltpu.SemaphoreType.DMA,
            pltpu.SemaphoreType.DMA((8,)),
            pltpu.SemaphoreType.DMA((8,)),
            pltpu.SemaphoreType.DMA((3, 3)),
            pltpu.SemaphoreType.DMA((len(PIECES), 6)),
            pltpu.SemaphoreType.DMA,
            pltpu.SemaphoreType.DMA,
        ],
        compiler_params=pltpu.CompilerParams(
            collective_id=0, has_side_effects=True, vmem_limit_bytes=32 << 20
        ),
    )(spectra)


def stack_kernel(rows_ref, cols_ref, g_ref, out_ref, held, sem):
    win = lax.axis_index("win")
    tiles = rows_ref.shape[0]
    norm = 1.0 / jnp.sqrt(jnp.float32(BLOCK))
    steps = tiles // UNROLL

    def put(f, step):
        slot = (f * steps + step) % 2
        return pltpu.make_async_copy(
            held.at[slot], out_ref.at[pl.ds(step * UNROLL, UNROLL), f], sem.at[slot]
        )

    for f in range(2):

        def body(step, carry):
            slot = (f * steps + step) % 2

            @pl.when(f * steps + step >= 2)
            def _():
                put(f, step).wait()

            for u in range(UNROLL):
                k = step * UNROLL + u
                turned = g_ref[rows_ref[k], f].T
                left = jnp.where(win == 0, turned[:64], turned[64:])
                crossed = jnp.concatenate([-left[:, 128:], left[:, :128]], axis=1)
                both = jnp.dot(
                    jnp.concatenate([left, crossed], axis=0),
                    g_ref[cols_ref[k], f],
                    preferred_element_type=jnp.float32,
                )
                both = both * norm
                held[slot, u, 0] = both[:64]
                held[slot, u, 1] = both[64:]
            put(f, step).start()
            return carry

        lax.fori_loop(0, steps, body, 0)
    put(1, steps - 2).wait()
    put(1, steps - 1).wait()


def stack_pairs(gathered, tile_rows, tile_cols):
    tiles = tile_rows.shape[0]
    return pl.pallas_call(
        stack_kernel,
        out_shape=jax.ShapeDtypeStruct((tiles, 2, 2, 64, BLOCK), jnp.float32),
        in_specs=[pl.BlockSpec(memory_space=pltpu.SMEM)] * 2 + [pl.BlockSpec(memory_space=pltpu.VMEM)],
        out_specs=pl.BlockSpec(memory_space=pl.ANY),
        scratch_shapes=[
            pltpu.VMEM((2, UNROLL, 2, 64, BLOCK), jnp.float32),
            pltpu.SemaphoreType.DMA((2,)),
        ],
        compiler_params=pltpu.CompilerParams(vmem_limit_bytes=30 << 20),
    )(tile_rows, tile_cols, gathered)


def on_device(spectra, tile_rows, tile_cols):
    values = spectra[0, :, 0].reshape(2, 2, BLOCK, BLOCK)
    gathered = gather(jnp.transpose(values, (0, 2, 1, 3)).reshape(2, 2 * BLOCK, BLOCK))
    return stack_pairs(gathered.reshape(BLOCK, 2, 2 * BLOCK, BLOCK), tile_rows, tile_cols)


def solution(mesh):
    in_specs = (P("win", None, ("row", "col"), None, None), P(("row", "col")), P(("row", "col")))
    out_specs = P(("row", "col"), None, None, "win", None)
    return jax.shard_map(
        on_device, mesh=mesh, in_specs=in_specs, out_specs=out_specs, check_vma=False
    )
```

time: 70.3 us -> 59.9 us (0.85)
  Pallas kernels: 67.7 us -> 58.8 us
  other arithmetic: 2.28 us -> 0 us
  local copies, waits for them, and re-layouts: 0.14 us -> 0.97 us
    pallas_call x1, Pallas kernels: 58.5 us -> 49.6 us  [gather(): pl.pallas_call(gather_kernel, out_shape=pltpu.VMEM(GATHERED, jnp.bfloat16...]
    reduce_sum x1 -> x0, other arithmetic: 1.18 us -> none  [whiten(): jnp.sum(spectra * spectra, axis=(1, 3), keepdims=True) / spectra.shape[1]]
    convert_element_type x1 -> x0, other arithmetic: 1.07 us -> none  [whiten(): (spectra / jnp.maximum(jnp.sqrt(power_sum), 1.0)).astype(jnp.bfloat16)]
    unnamed x4 -> x6, local copies, waits for them, and re-layouts: 0.01 us -> 0.97 us
where the time goes in v2:
time: 59.9 us; the launch traced here: 59.8 us
  Pallas kernels  58.8 us (98%)
  local copies, waits for them, and re-layouts  0.97 us (2%)
    pallas_call x1, Pallas kernels, gather(): pl.pallas_call(gather_kernel, out_shape=pltpu.VMEM(GATHERED, jnp.bfloat16...  49.6 us
    pallas_call x1, Pallas kernels, stack_pairs(): pl.pallas_call(stack_kernel, out_shape=jax.ShapeDtypeStruct((tiles, 2, 2,...  9.19 us

profile of v2, /device:TPU:1, one launch (start us, length us, event | category | flops | bytes accessed | tf_op | source)
XLA Modules:
  0.0 59.8 jit_solution(10171848460980102292)
XLA Ops:
  0.0 0.0 copy-start.1
  0.0 0.0 copy-start
  0.0 1.0 %copy-done = f32[1,2,1,2,16384]{4,3,2,1,0:T(2,128)S(1)} copy-done((f32[1,2,1,2,16384]{4,3,2,1,0:T(2,128)S(1)}, f32[1,2,1,2,16384]{4,3,2,1,0:T(2,128)}, u32[]{:S(2)}) %copy-start) | copy-done | bytes 262168
  1.0 0.0 copy-start.2
  1.0 49.6 %shard_map.37 = bf16[2,4,32,2,4,4,8,128]{7,6,5,4,3,2,1,0:T(8,128)(2,1)S(1)} custom-call(f32[2,256,128]{2,1,0:T(8,128)S(1)} %bitcast.7), custom_call_target="tpu_custom_call" | custom-call | tf_op jit(solution)/shard_map/pallas_call | solution.py:201
  50.6 0.0 copy-done.1
  50.6 0.0 copy-done.2
  50.6 9.2 %shard_map.38 = f32[129,2,2,64,128]{4,3,2,1,0:T(8,128)} custom-call(s32[129]{0:T(256)S(1)} %copy-done.1, s32[129]{0:T(256)S(1)} %copy-done.2, bf16[128,2,256,128]{3,2,1,0:T(8,128)(2,1)S(1)} %bitcast.6), custom_call_target="tpu_custom_call" | custom-call | tf_op jit(solution)/shard_map/pallas_call | solution.py:269
Async XLA Ops:
  0.0 50.6 %copy-start.1 = (s32[129]{0:T(256)S(1)}, s32[129]{0:T(256)}, u32[]{:S(2)}) copy-start(s32[129]{0:T(256)} %rows_ref.1) | copy-start | bytes 1552
  0.0 1.0 %copy-start = (f32[1,2,1,2,16384]{4,3,2,1,0:T(2,128)S(1)}, f32[1,2,1,2,16384]{4,3,2,1,0:T(2,128)}, u32[]{:S(2)}) copy-start(f32[1,2,1,2,16384]{4,3,2,1,0:T(2,128)} %param.3) | copy-start | bytes 786436
  1.0 49.6 %copy-start.2 = (s32[129]{0:T(256)S(1)}, s32[129]{0:T(256)}, u32[]{:S(2)}) copy-start(s32[129]{0:T(256)} %cols_ref.1) | copy-start | bytes 1552

commit v3 on v2

--- a/solution.py
+++ b/solution.py
@@ -14,36 +14,47 @@
 STREAMS = ((0, 11, "xyz"), (11, 11, "yzx"), (22, 10, "zxy"))
 OFFSETS = (0, 1, -1, 2)
 SLOTS = ((1, 0, 0), (-1, 0, 1), (1, 0, 1), (-1, 0, 0), (1, -1, 0), (-1, 1, 1))
-PIECES = tuple(
-    (stream, phase, offset)
-    for stream in range(3)
-    for phase in range(3)
-    for offset in (OFFSETS if phase else (0,))
-)
-UNROLL = 43
+
+
+def cut_pieces(last=3):
+    pieces = []
+    for stream, (first, units, _) in enumerate(STREAMS):
+        pieces.append((stream, 0, 0, None, first, units))
+        for offset in OFFSETS:
+            pieces.append((stream, 1, offset, None, first, units))
+        for offset in OFFSETS:
+            for before in OFFSETS if offset == 0 else (None,):
+                parts = last if offset == 2 else 1
+                edges = [first + units * i // parts for i in range(parts + 1)]
+                for lo, hi in zip(edges, edges[1:]):
+                    pieces.append((stream, 2, offset, before, lo, hi - lo))
+    return tuple(pieces)
+
+
+PIECES = cut_pieces()
+CUTS = (5, 12, 20, 24, 24, 20, 14, 10)
 
 
 def plan(hop=1.6, rate=46.5e3):
     needs = {}
     for piece in PIECES:
-        stream, phase, offset = piece
+        stream, phase, offset, before = piece[:4]
         for part in range(2):
-            if phase == 0 or (phase == 1 and offset == 0):
+            if phase == 1 and offset:
+                need = {(stream, 0, 0, offset, part)}
+            elif phase == 2 and offset:
+                need = {(stream, 1, by, offset, part) for by in OFFSETS}
+            elif phase == 2 and before:
+                need = {(stream, 0, 0, before, part)}
+            else:
                 need = set()
-            elif phase == 1:
-                need = {((stream, 0, 0), offset, part)}
-            elif offset == 0:
-                need = {((stream, 0, 0), by, part) for by in OFFSETS[1:]}
-            else:
-                need = {((stream, 1, by), offset, part) for by in OFFSETS}
             needs[piece, part] = need
     free, heap, have, started = {}, [], set(), set()
 
     def send(piece, slot, now):
-        stream, phase, offset = piece
-        _, units, order = STREAMS[stream]
-        link = (order[phase], SLOTS[slot][0])
-        size = units * 2048 * (4 if phase == 2 else 1)
+        stream, phase, _, before, _, units = piece
+        link = (STREAMS[stream][2][phase], SLOTS[slot][0])
+        size = units * 2048 * (4 if phase == 2 and before is None else 1)
         begin = max(now, free.get(link, 0.0))
         free[link] = begin + size / rate
         heapq.heappush(heap, (free[link] + hop, len(started), piece, slot))
@@ -68,7 +79,7 @@
         if slot < 2:
             send(piece, slot + 4, now)
             out.append((piece, slot + 4))
-        have.add((piece, {-1: -1, 1: 1, -2: 2, 2: 2}[whose - way], part))
+        have.add((*piece[:3], {-1: -1, 1: 1, -2: 2, 2: 2}[whose - way], part))
         steps.append(((piece, slot), out + ready(now)))
     return steps, now
 
@@ -140,14 +151,14 @@
     every = slice(None)
 
     def box(piece, by, part):
-        stream, phase, offset = piece
-        first, units, order = STREAMS[stream]
+        stream, phase, offset, before, first, units = piece
+        order = STREAMS[stream][2]
         at = dict(here)
         at[order[phase]] = (here[order[phase]] + by) % 4
         if phase:
             at[order[phase - 1]] = (here[order[phase - 1]] + offset) % 4
         if phase == 2:
-            at[order[0]] = every
+            at[order[0]] = every if before is None else (here[order[0]] + before) % 4
         return g.at[core, at["y"], pl.ds(first, units), part, at["x"], at["z"]]
 
     def index(piece):
@@ -224,27 +235,12 @@
 
 def stack_kernel(rows_ref, cols_ref, g_ref, out_ref, held, sem):
     win = lax.axis_index("win")
-    tiles = rows_ref.shape[0]
     norm = 1.0 / jnp.sqrt(jnp.float32(BLOCK))
-    steps = tiles // UNROLL
-
-    def put(f, step):
-        slot = (f * steps + step) % 2
-        return pltpu.make_async_copy(
-            held.at[slot], out_ref.at[pl.ds(step * UNROLL, UNROLL), f], sem.at[slot]
-        )
-
+    puts = []
     for f in range(2):
-
-        def body(step, carry):
-            slot = (f * steps + step) % 2
-
-            @pl.when(f * steps + step >= 2)
-            def _():
-                put(f, step).wait()
-
-            for u in range(UNROLL):
-                k = step * UNROLL + u
+        first = 0
+        for tiles in CUTS if f == 0 else CUTS[::-1]:
+            for k in range(first, first + tiles):
                 turned = g_ref[rows_ref[k], f].T
                 left = jnp.where(win == 0, turned[:64], turned[64:])
                 crossed = jnp.concatenate([-left[:, 128:], left[:, :128]], axis=1)
@@ -254,14 +250,16 @@
                     preferred_element_type=jnp.float32,
                 )
                 both = both * norm
-                held[slot, u, 0] = both[:64]
-                held[slot, u, 1] = both[64:]
-            put(f, step).start()
-            return carry
-
-        lax.fori_loop(0, steps, body, 0)
-    put(1, steps - 2).wait()
-    put(1, steps - 1).wait()
+                held[f, k, 0] = both[:64]
+                held[f, k, 1] = both[64:]
+            put = pltpu.make_async_copy(
+                held.at[f, pl.ds(first, tiles)], out_ref.at[pl.ds(first, tiles), f], sem.at[len(puts)]
+            )
+            put.start()
+            puts.append(put)
+            first += tiles
+    for put in puts:
+        put.wait()
 
 
 def stack_pairs(gathered, tile_rows, tile_cols):
@@ -272,16 +270,17 @@
         in_specs=[pl.BlockSpec(memory_space=pltpu.SMEM)] * 2 + [pl.BlockSpec(memory_space=pltpu.VMEM)],
         out_specs=pl.BlockSpec(memory_space=pl.ANY),
         scratch_shapes=[
-            pltpu.VMEM((2, UNROLL, 2, 64, BLOCK), jnp.float32),
-            pltpu.SemaphoreType.DMA((2,)),
+            pltpu.VMEM((2, tiles, 2, 64, BLOCK), jnp.float32),
+            pltpu.SemaphoreType.DMA((2 * len(CUTS),)),
         ],
-        compiler_params=pltpu.CompilerParams(vmem_limit_bytes=30 << 20),
+        compiler_params=pltpu.CompilerParams(vmem_limit_bytes=24 << 20),
     )(tile_rows, tile_cols, gathered)
 
 
 def on_device(spectra, tile_rows, tile_cols):
     values = spectra[0, :, 0].reshape(2, 2, BLOCK, BLOCK)
-    gathered = gather(jnp.transpose(values, (0, 2, 1, 3)).reshape(2, 2 * BLOCK, BLOCK))
+    values = jnp.transpose(values, (0, 2, 1, 3)).reshape(2, 2 * BLOCK, BLOCK)
+    gathered = gather(pltpu.with_memory_space_constraint(values, pltpu.HBM))
     return stack_pairs(gathered.reshape(BLOCK, 2, 2 * BLOCK, BLOCK), tile_rows, tile_cols)
 
 

time: 59.9 us -> 56 us (0.935)
  Pallas kernels: 58.8 us -> 55.9 us
  local copies, waits for them, and re-layouts: 0.97 us -> 0.01 us
    pallas_call x1, Pallas kernels: 9.19 us -> 7.1 us  [stack_pairs(): pl.pallas_call(stack_kernel, out_shape=jax.ShapeDtypeStruct((tiles, 2, 2,...]
    unnamed x6 -> x4, local copies, waits for them, and re-layouts: 0.97 us -> 0.01 us
    pallas_call x1, Pallas kernels: 49.6 us -> 48.8 us  [gather(): pl.pallas_call(gather_kernel, out_shape=pltpu.VMEM(GATHERED, jnp.bfloat16...]
where the time goes in v3:
time: 56 us; the launch traced here: 55.9 us
  Pallas kernels  55.9 us (100%)
    pallas_call x1, Pallas kernels, gather(): pl.pallas_call(gather_kernel, out_shape=pltpu.VMEM(GATHERED, jnp.bfloat16...  48.8 us
    pallas_call x1, Pallas kernels, stack_pairs(): pl.pallas_call(stack_kernel, out_shape=jax.ShapeDtypeStruct((tiles, 2, 2,...  7.1 us

profile of v3, /device:TPU:1, one launch (start us, length us, event | category | flops | bytes accessed | tf_op | source)
XLA Modules:
  0.0 55.9 jit_solution(14604244716430436353)
XLA Ops:
  0.0 0.0 copy-start.1
  0.0 0.0 copy-start
  0.0 48.8 %shard_map.37 = bf16[2,4,32,2,4,4,8,128]{7,6,5,4,3,2,1,0:T(8,128)(2,1)S(1)} custom-call(f32[2,256,128]{2,1,0:T(8,128)} %bitcast.7), custom_call_target="tpu_custom_call" | custom-call | tf_op jit(solution)/shard_map/pallas_call | solution.py:212
  48.8 0.0 copy-done.1
  48.8 0.0 copy-done
  48.8 7.1 %shard_map.38 = f32[129,2,2,64,128]{4,3,2,1,0:T(8,128)} custom-call(s32[129]{0:T(256)S(1)} %copy-done, s32[129]{0:T(256)S(1)} %copy-done.1, bf16[128,2,256,128]{3,2,1,0:T(8,128)(2,1)S(1)} %bitcast.6), custom_call_target="tpu_custom_call" | custom-call | tf_op jit(solution)/shard_map/pallas_call | solution.py:267
Async XLA Ops:
  0.0 48.8 %copy-start.1 = (s32[129]{0:T(256)S(1)}, s32[129]{0:T(256)}, u32[]{:S(2)}) copy-start(s32[129]{0:T(256)} %cols_ref.1) | copy-start | bytes 1552
  0.0 48.8 %copy-start = (s32[129]{0:T(256)S(1)}, s32[129]{0:T(256)}, u32[]{:S(2)}) copy-start(s32[129]{0:T(256)} %rows_ref.1) | copy-start | bytes 1552

commit v4 on v3

--- a/solution.py
+++ b/solution.py
@@ -1,5 +1,6 @@
-import functools
 import heapq
+import itertools
+import math
 
 import jax
 import jax.numpy as jnp
@@ -16,29 +17,48 @@
 SLOTS = ((1, 0, 0), (-1, 0, 1), (1, 0, 1), (-1, 0, 0), (1, -1, 0), (-1, 1, 1))
 
 
-def cut_pieces(last=3):
+def cut_pieces():
     pieces = []
-    for stream, (first, units, _) in enumerate(STREAMS):
-        pieces.append((stream, 0, 0, None, first, units))
-        for offset in OFFSETS:
-            pieces.append((stream, 1, offset, None, first, units))
-        for offset in OFFSETS:
-            for before in OFFSETS if offset == 0 else (None,):
-                parts = last if offset == 2 else 1
-                edges = [first + units * i // parts for i in range(parts + 1)]
-                for lo, hi in zip(edges, edges[1:]):
-                    pieces.append((stream, 2, offset, before, lo, hi - lo))
+    for stream in range(len(STREAMS)):
+        pieces.append((stream, 0, 0, None))
+        pieces += [(stream, 1, offset, None) for offset in OFFSETS]
+        pieces += [(stream, 2, 0, before) for before in OFFSETS]
+        pieces += [(stream, 2, offset, None) for offset in OFFSETS[1:]]
     return tuple(pieces)
 
 
+def group_of(piece, slot):
+    stream, phase, offset, before = piece
+    if slot < 2:
+        return (piece, slot)
+    if phase == 0:
+        return (piece, min(slot, 4))
+    if phase == 1:
+        return (stream, 1, slot // 2)
+    if offset == 0 and before:
+        return (stream, 2)
+    if offset == 2:
+        return (piece, slot // 2)
+    return (piece, 2)
+
+
 PIECES = cut_pieces()
+GROUPS = {}
+for _piece in PIECES:
+    for _slot in range(6):
+        GROUPS.setdefault(group_of(_piece, _slot), []).append((_piece, _slot))
+ORDER = list(GROUPS)
 CUTS = (5, 12, 20, 24, 24, 20, 14, 10)
 
 
-def plan(hop=1.6, rate=46.5e3):
+def group_stream(group):
+    return GROUPS[group][0][0][0]
+
+
+def plan(hop=3.5, rate=46.5e3):
     needs = {}
     for piece in PIECES:
-        stream, phase, offset, before = piece[:4]
+        stream, phase, offset, before = piece
         for part in range(2):
             if phase == 1 and offset:
                 need = {(stream, 0, 0, offset, part)}
@@ -50,11 +70,12 @@
                 need = set()
             needs[piece, part] = need
     free, heap, have, started = {}, [], set(), set()
+    missing = {group: len(copies) for group, copies in GROUPS.items()}
 
     def send(piece, slot, now):
-        stream, phase, _, before, _, units = piece
+        stream, phase, _, before = piece
         link = (STREAMS[stream][2][phase], SLOTS[slot][0])
-        size = units * 2048 * (4 if phase == 2 and before is None else 1)
+        size = STREAMS[stream][1] * 2048 * (4 if phase == 2 and before is None else 1)
         begin = max(now, free.get(link, 0.0))
         free[link] = begin + size / rate
         heapq.heappush(heap, (free[link] + hop, len(started), piece, slot))
@@ -74,13 +95,18 @@
     steps = [(None, ready(0.0))]
     while heap:
         now, _, piece, slot = heapq.heappop(heap)
-        way, whose, part = SLOTS[slot]
+        group = group_of(piece, slot)
+        missing[group] -= 1
+        if missing[group]:
+            continue
         out = []
-        if slot < 2:
-            send(piece, slot + 4, now)
-            out.append((piece, slot + 4))
-        have.add((*piece[:3], {-1: -1, 1: 1, -2: 2, 2: 2}[whose - way], part))
-        steps.append(((piece, slot), out + ready(now)))
+        for piece, slot in GROUPS[group]:
+            way, whose, part = SLOTS[slot]
+            if slot < 2:
+                send(piece, slot + 4, now)
+                out.append((piece, slot + 4))
+            have.add((*piece[:3], {-1: -1, 1: 1, -2: 2, 2: 2}[whose - way], part))
+        steps.append((group, out + ready(now)))
     return steps, now
 
 
@@ -105,10 +131,21 @@
     fetch = pltpu.make_async_copy(x_ref, raw, load)
     fetch.start()
     barrier = pltpu.get_barrier_semaphore()
-    others = [member(by)[1] for by in range(1, 8)]
-    others += [device(shifted(axis, by), core) for axis in "xz" for by in (1, -1)]
-    for other in others:
+
+    def greet(other):
         pl.semaphore_signal(barrier, inc=1, device_id=other, device_id_type=MESH)
+
+    def greet_member(by, carry):
+        greet(member(by)[1])
+        return carry
+
+    def greet_neighbours(i, carry):
+        greet(device(shifted("x", 1 + 2 * i), core))
+        greet(device(shifted("z", 1 + 2 * i), core))
+        return carry
+
+    lax.fori_loop(1, 8, greet_member, 0)
+    lax.fori_loop(0, 2, greet_neighbours, 0)
     fetch.wait()
     for m in range(8):
         values = [[raw[f, pl.ds(m * 32 + p, 16, stride=2), :] for p in range(2)] for f in range(2)]
@@ -117,27 +154,29 @@
         for f in range(2):
             for p in range(2):
                 source[m, f, p] = (values[f][p] / scale).astype(jnp.bfloat16)
-    pl.semaphore_wait(barrier, len(others))
+    pl.semaphore_wait(barrier, 11)
 
     def swap(by):
         m, where = member(by)
         return pltpu.make_async_remote_copy(
             src_ref=source.at[m],
             dst_ref=landed.at[me],
-            send_sem=a2a_send.at[by],
-            recv_sem=a2a_recv.at[by],
+            send_sem=a2a_send,
+            recv_sem=a2a_recv,
             device_id=where,
             device_id_type=MESH,
         )
 
-    swaps = [swap(by) for by in range(1, 8)]
-    for copy in swaps:
-        copy.start()
-    own = pltpu.make_async_copy(source.at[me], landed.at[me], a2a_recv.at[0])
+    def start_swap(by, carry):
+        swap(by).start()
+        return carry
+
+    lax.fori_loop(1, 8, start_swap, 0)
+    own = pltpu.make_async_copy(source.at[me], landed.at[me], load)
     own.start()
     own.wait()
-    for copy in swaps:
-        copy.wait_recv()
+    seven = landed.at[pl.ds(0, 7)]
+    pltpu.make_async_copy(seven, seven, a2a_recv).wait()
     for f in range(2):
         for p in range(2):
             for s in range(8):
@@ -151,8 +190,8 @@
     every = slice(None)
 
     def box(piece, by, part):
-        stream, phase, offset, before, first, units = piece
-        order = STREAMS[stream][2]
+        stream, phase, offset, before = piece
+        first, units, order = STREAMS[stream]
         at = dict(here)
         at[order[phase]] = (here[order[phase]] + by) % 4
         if phase:
@@ -161,8 +200,14 @@
             at[order[0]] = every if before is None else (here[order[0]] + before) % 4
         return g.at[core, at["y"], pl.ds(first, units), part, at["x"], at["z"]]
 
-    def index(piece):
-        return PIECES.index(piece)
+    def any_boxes(stream, count):
+        first, units, _ = STREAMS[stream]
+        ys, xs, zs, parts = next(
+            dims
+            for dims in itertools.product(range(1, 5), range(1, 5), range(1, 5), (1, 2))
+            if math.prod(dims) == count
+        )
+        return g.at[core, pl.ds(0, ys), pl.ds(first, units), pl.ds(0, parts), pl.ds(0, xs), pl.ds(0, zs)]
 
     def launch(piece, slot):
         way, whose, part = SLOTS[slot]
@@ -171,7 +216,7 @@
             src_ref=ref,
             dst_ref=ref,
             send_sem=sent.at[piece[0], piece[1]],
-            recv_sem=got.at[index(piece), slot],
+            recv_sem=got.at[ORDER.index(group_of(piece, slot))],
             device_id=device(shifted(STREAMS[piece[0]][2][piece[1]], way), core),
             device_id_type=MESH,
         ).start()
@@ -186,18 +231,22 @@
             device_id_type=MESH,
         ).start()
 
-    for received, copies in plan()[0]:
-        if received is not None:
-            piece, slot = received
-            way, whose, part = SLOTS[slot]
-            ref = box(piece, whose - way, part)
-            pltpu.make_async_copy(ref, ref, got.at[index(piece), slot]).wait()
+    for group, copies in plan()[0]:
+        refs = [g.at[core, y, :, :, x, z]]
+        if group is not None:
+            refs, count = [], 0
+            for piece, slot in GROUPS[group]:
+                way, whose, part = SLOTS[slot]
+                refs.append(box(piece, whose - way, part))
+                count += 4 if piece[1] == 2 and piece[3] is None else 1
+            ref = refs[0] if len(refs) == 1 else any_boxes(group_stream(group), count)
+            pltpu.make_async_copy(ref, ref, got.at[ORDER.index(group)]).wait()
         for copy in copies:
             launch(*copy)
-        hand_over(g.at[core, y, :, :, x, z] if received is None else ref)
-
-    for copy in swaps:
-        copy.wait_send()
+        for ref in refs:
+            hand_over(ref)
+
+    pltpu.make_async_copy(seven, seven, a2a_send).wait()
     for s, (first, units, _) in enumerate(STREAMS):
         for phase in range(3):
             xs = slice(0, 1) if phase == 0 else every
@@ -220,10 +269,10 @@
             pltpu.VMEM((8, 2, 2, 16, BLOCK), jnp.bfloat16),
             pltpu.VMEM((2, 2, BLOCK, BLOCK), jnp.float32),
             pltpu.SemaphoreType.DMA,
-            pltpu.SemaphoreType.DMA((8,)),
-            pltpu.SemaphoreType.DMA((8,)),
+            pltpu.SemaphoreType.DMA,
+            pltpu.SemaphoreType.DMA,
             pltpu.SemaphoreType.DMA((3, 3)),
-            pltpu.SemaphoreType.DMA((len(PIECES), 6)),
+            pltpu.SemaphoreType.DMA((len(ORDER),)),
             pltpu.SemaphoreType.DMA,
             pltpu.SemaphoreType.DMA,
         ],
@@ -236,7 +285,6 @@
 def stack_kernel(rows_ref, cols_ref, g_ref, out_ref, held, sem):
     win = lax.axis_index("win")
     norm = 1.0 / jnp.sqrt(jnp.float32(BLOCK))
-    puts = []
     for f in range(2):
         first = 0
         for tiles in CUTS if f == 0 else CUTS[::-1]:
@@ -253,13 +301,11 @@
                 held[f, k, 0] = both[:64]
                 held[f, k, 1] = both[64:]
             put = pltpu.make_async_copy(
-                held.at[f, pl.ds(first, tiles)], out_ref.at[pl.ds(first, tiles), f], sem.at[len(puts)]
+                held.at[f, pl.ds(first, tiles)], out_ref.at[pl.ds(first, tiles), f], sem
             )
             put.start()
-            puts.append(put)
             first += tiles
-    for put in puts:
-        put.wait()
+    pltpu.make_async_copy(held, held, sem).wait()
 
 
 def stack_pairs(gathered, tile_rows, tile_cols):
@@ -271,7 +317,7 @@
         out_specs=pl.BlockSpec(memory_space=pl.ANY),
         scratch_shapes=[
             pltpu.VMEM((2, tiles, 2, 64, BLOCK), jnp.float32),
-            pltpu.SemaphoreType.DMA((2 * len(CUTS),)),
+            pltpu.SemaphoreType.DMA,
         ],
         compiler_params=pltpu.CompilerParams(vmem_limit_bytes=24 << 20),
     )(tile_rows, tile_cols, gathered)

time: 56 us -> 54.7 us (0.977)
  Pallas kernels: 55.9 us -> 54.5 us
    pallas_call x1, Pallas kernels: 48.8 us -> 47.6 us  [gather(): pl.pallas_call(gather_kernel, out_shape=pltpu.VMEM(GATHERED, jnp.bfloat16...]
where the time goes in v4:
time: 54.7 us; the launch traced here: 54.6 us
  Pallas kernels  54.5 us (100%)
    pallas_call x1, Pallas kernels, gather(): pl.pallas_call(gather_kernel, out_shape=pltpu.VMEM(GATHERED, jnp.bfloat16...  47.6 us
    pallas_call x1, Pallas kernels, stack_pairs(): pl.pallas_call(stack_kernel, out_shape=jax.ShapeDtypeStruct((tiles, 2, 2,...  6.97 us

profile of v4, /device:TPU:1, one launch (start us, length us, event | category | flops | bytes accessed | tf_op | source)
XLA Modules:
  0.0 54.6 jit_solution(6110672533064695423)
XLA Ops:
  0.0 0.0 copy-start.1
  0.0 0.0 copy-start
  0.0 47.6 %shard_map.37 = bf16[2,4,32,2,4,4,8,128]{7,6,5,4,3,2,1,0:T(8,128)(2,1)S(1)} custom-call(f32[2,256,128]{2,1,0:T(8,128)} %bitcast.7), custom_call_target="tpu_custom_call" | custom-call | tf_op jit(solution)/shard_map/pallas_call | solution.py:261
  47.6 0.0 copy-done.1
  47.6 0.0 copy-done
  47.6 7.0 %shard_map.38 = f32[129,2,2,64,128]{4,3,2,1,0:T(8,128)} custom-call(s32[129]{0:T(256)S(1)} %copy-done, s32[129]{0:T(256)S(1)} %copy-done.1, bf16[128,2,256,128]{3,2,1,0:T(8,128)(2,1)S(1)} %bitcast.6), custom_call_target="tpu_custom_call" | custom-call | tf_op jit(solution)/shard_map/pallas_call | solution.py:313
Async XLA Ops:
  0.0 47.6 %copy-start.1 = (s32[129]{0:T(256)S(1)}, s32[129]{0:T(256)}, u32[]{:S(2)}) copy-start(s32[129]{0:T(256)} %cols_ref.1) | copy-start | bytes 1552
  0.0 47.6 %copy-start = (s32[129]{0:T(256)S(1)}, s32[129]{0:T(256)}, u32[]{:S(2)}) copy-start(s32[129]{0:T(256)} %rows_ref.1) | copy-start | bytes 1552

commit v5 on v4

--- a/solution.py
+++ b/solution.py
@@ -17,18 +17,20 @@
 SLOTS = ((1, 0, 0), (-1, 0, 1), (1, 0, 1), (-1, 0, 0), (1, -1, 0), (-1, 1, 1))
 
 
-def cut_pieces():
+def cut_pieces(last=3):
     pieces = []
-    for stream in range(len(STREAMS)):
-        pieces.append((stream, 0, 0, None))
-        pieces += [(stream, 1, offset, None) for offset in OFFSETS]
-        pieces += [(stream, 2, 0, before) for before in OFFSETS]
-        pieces += [(stream, 2, offset, None) for offset in OFFSETS[1:]]
-    return tuple(pieces)
+    for stream, (first, units, _) in enumerate(STREAMS):
+        pieces.append((stream, 0, 0, None, first, units))
+        pieces += [(stream, 1, offset, None, first, units) for offset in OFFSETS]
+        pieces += [(stream, 2, 0, before, first, units) for before in OFFSETS]
+        pieces += [(stream, 2, offset, None, first, units) for offset in (1, -1)]
+        cut = units - last
+        pieces += [(stream, 2, 2, None, first, cut), (stream, 2, 2, None, first + cut, last)]
+    return tuple(p for p in pieces if p[5])
 
 
 def group_of(piece, slot):
-    stream, phase, offset, before = piece
+    stream, phase, offset, before = piece[:4]
     if slot < 2:
         return (piece, slot)
     if phase == 0:
@@ -51,14 +53,10 @@
 CUTS = (5, 12, 20, 24, 24, 20, 14, 10)
 
 
-def group_stream(group):
-    return GROUPS[group][0][0][0]
-
-
 def plan(hop=3.5, rate=46.5e3):
     needs = {}
     for piece in PIECES:
-        stream, phase, offset, before = piece
+        stream, phase, offset, before = piece[:4]
         for part in range(2):
             if phase == 1 and offset:
                 need = {(stream, 0, 0, offset, part)}
@@ -73,9 +71,9 @@
     missing = {group: len(copies) for group, copies in GROUPS.items()}
 
     def send(piece, slot, now):
-        stream, phase, _, before = piece
+        stream, phase, _, before, _, units = piece
         link = (STREAMS[stream][2][phase], SLOTS[slot][0])
-        size = STREAMS[stream][1] * 2048 * (4 if phase == 2 and before is None else 1)
+        size = units * 2048 * (4 if phase == 2 and before is None else 1)
         begin = max(now, free.get(link, 0.0))
         free[link] = begin + size / rate
         heapq.heappush(heap, (free[link] + hop, len(started), piece, slot))
@@ -167,11 +165,8 @@
             device_id_type=MESH,
         )
 
-    def start_swap(by, carry):
+    for by in (2, 6, 1, 5, 3, 7, 4):
         swap(by).start()
-        return carry
-
-    lax.fori_loop(1, 8, start_swap, 0)
     own = pltpu.make_async_copy(source.at[me], landed.at[me], load)
     own.start()
     own.wait()
@@ -190,8 +185,8 @@
     every = slice(None)
 
     def box(piece, by, part):
-        stream, phase, offset, before = piece
-        first, units, order = STREAMS[stream]
+        stream, phase, offset, before, first, units = piece
+        order = STREAMS[stream][2]
         at = dict(here)
         at[order[phase]] = (here[order[phase]] + by) % 4
         if phase:
@@ -200,8 +195,8 @@
             at[order[0]] = every if before is None else (here[order[0]] + before) % 4
         return g.at[core, at["y"], pl.ds(first, units), part, at["x"], at["z"]]
 
-    def any_boxes(stream, count):
-        first, units, _ = STREAMS[stream]
+    def any_boxes(piece, count):
+        first, units = piece[4:]
         ys, xs, zs, parts = next(
             dims
             for dims in itertools.product(range(1, 5), range(1, 5), range(1, 5), (1, 2))
@@ -239,7 +234,7 @@
                 way, whose, part = SLOTS[slot]
                 refs.append(box(piece, whose - way, part))
                 count += 4 if piece[1] == 2 and piece[3] is None else 1
-            ref = refs[0] if len(refs) == 1 else any_boxes(group_stream(group), count)
+            ref = refs[0] if len(refs) == 1 else any_boxes(GROUPS[group][0][0], count)
             pltpu.make_async_copy(ref, ref, got.at[ORDER.index(group)]).wait()
         for copy in copies:
             launch(*copy)

time: 54.7 us -> 54 us (0.987)
  Pallas kernels: 54.5 us -> 53.9 us
    pallas_call x1, Pallas kernels: 47.6 us -> 46.9 us  [gather(): pl.pallas_call(gather_kernel, out_shape=pltpu.VMEM(GATHERED, jnp.bfloat16...]
where the time goes in v5:
time: 54 us; the launch traced here: 53.9 us
  Pallas kernels  53.9 us (100%)
    pallas_call x1, Pallas kernels, gather(): pl.pallas_call(gather_kernel, out_shape=pltpu.VMEM(GATHERED, jnp.bfloat16...  46.9 us
    pallas_call x1, Pallas kernels, stack_pairs(): pl.pallas_call(stack_kernel, out_shape=jax.ShapeDtypeStruct((tiles, 2, 2,...  6.97 us

profile of v5, /device:TPU:1, one launch (start us, length us, event | category | flops | bytes accessed | tf_op | source)
XLA Modules:
  0.0 53.9 jit_solution(15388286826553748868)
XLA Ops:
  0.0 0.0 copy-start.1
  0.0 0.0 copy-start
  0.0 46.9 %shard_map.37 = bf16[2,4,32,2,4,4,8,128]{7,6,5,4,3,2,1,0:T(8,128)(2,1)S(1)} custom-call(f32[2,256,128]{2,1,0:T(8,128)} %bitcast.7), custom_call_target="tpu_custom_call" | custom-call | tf_op jit(solution)/shard_map/pallas_call | solution.py:256
  46.9 0.0 copy-done.1
  47.0 0.0 copy-done
  47.0 7.0 %shard_map.38 = f32[129,2,2,64,128]{4,3,2,1,0:T(8,128)} custom-call(s32[129]{0:T(256)S(1)} %copy-done, s32[129]{0:T(256)S(1)} %copy-done.1, bf16[128,2,256,128]{3,2,1,0:T(8,128)(2,1)S(1)} %bitcast.6), custom_call_target="tpu_custom_call" | custom-call | tf_op jit(solution)/shard_map/pallas_call | solution.py:308
Async XLA Ops:
  0.0 46.9 %copy-start.1 = (s32[129]{0:T(256)S(1)}, s32[129]{0:T(256)}, u32[]{:S(2)}) copy-start(s32[129]{0:T(256)} %cols_ref.1) | copy-start | bytes 1552
  0.0 46.9 %copy-start = (s32[129]{0:T(256)S(1)}, s32[129]{0:T(256)}, u32[]{:S(2)}) copy-start(s32[129]{0:T(256)} %rows_ref.1) | copy-start | bytes 1552

commit v6 on v5

--- a/solution.py
+++ b/solution.py
@@ -12,7 +12,7 @@
 MESH = pl.DeviceIdType.MESH
 BLOCK = 128
 GATHERED = (2, 4, 32, 2, 4, 4, 8, BLOCK)
-STREAMS = ((0, 11, "xyz"), (11, 11, "yzx"), (22, 10, "zxy"))
+STREAMS = ((0, 10, "xyz"), (10, 11, "yzx"), (21, 11, "zxy"))
 OFFSETS = (0, 1, -1, 2)
 SLOTS = ((1, 0, 0), (-1, 0, 1), (1, 0, 1), (-1, 0, 0), (1, -1, 0), (-1, 1, 1))
 
@@ -31,7 +31,7 @@
 
 def group_of(piece, slot):
     stream, phase, offset, before = piece[:4]
-    if slot < 2:
+    if slot < 2 or (phase == 2 and offset):
         return (piece, slot)
     if phase == 0:
         return (piece, min(slot, 4))
@@ -39,8 +39,6 @@
         return (stream, 1, slot // 2)
     if offset == 0 and before:
         return (stream, 2)
-    if offset == 2:
-        return (piece, slot // 2)
     return (piece, 2)
 
 

time: 54 us -> 54 us (level)
  no operation moved by 1% of the time
where the time goes in v6:
time: 54 us; the launch traced here: 53.9 us
  Pallas kernels  53.8 us (100%)
    pallas_call x1, Pallas kernels, gather(): pl.pallas_call(gather_kernel, out_shape=pltpu.VMEM(GATHERED, jnp.bfloat16...  46.9 us
    pallas_call x1, Pallas kernels, stack_pairs(): pl.pallas_call(stack_kernel, out_shape=jax.ShapeDtypeStruct((tiles, 2, 2,...  6.97 us

profile of v6, /device:TPU:1, one launch (start us, length us, event | category | flops | bytes accessed | tf_op | source)
XLA Modules:
  0.0 53.9 jit_solution(3241051245950653598)
XLA Ops:
  0.0 0.0 copy-start.1
  0.0 0.0 copy-start
  0.0 46.9 %shard_map.37 = bf16[2,4,32,2,4,4,8,128]{7,6,5,4,3,2,1,0:T(8,128)(2,1)S(1)} custom-call(f32[2,256,128]{2,1,0:T(8,128)} %bitcast.7), custom_call_target="tpu_custom_call" | custom-call | tf_op jit(solution)/shard_map/pallas_call | solution.py:254
  46.9 0.0 copy-done.1
  46.9 0.0 copy-done
  46.9 7.0 %shard_map.38 = f32[129,2,2,64,128]{4,3,2,1,0:T(8,128)} custom-call(s32[129]{0:T(256)S(1)} %copy-done, s32[129]{0:T(256)S(1)} %copy-done.1, bf16[128,2,256,128]{3,2,1,0:T(8,128)(2,1)S(1)} %bitcast.6), custom_call_target="tpu_custom_call" | custom-call | tf_op jit(solution)/shard_map/pallas_call | solution.py:306
Async XLA Ops:
  0.0 46.9 %copy-start.1 = (s32[129]{0:T(256)S(1)}, s32[129]{0:T(256)}, u32[]{:S(2)}) copy-start(s32[129]{0:T(256)} %cols_ref.1) | copy-start | bytes 1552
  0.0 46.9 %copy-start = (s32[129]{0:T(256)S(1)}, s32[129]{0:T(256)}, u32[]{:S(2)}) copy-start(s32[129]{0:T(256)} %rows_ref.1) | copy-start | bytes 1552
